TPU v7x, 256 devices: a whole 4x4x8 slice. The times are simulated.
256 devices in a mesh: depth: 4 (over z_hi), row: 16 (over x, y), col: 4 (over z_lo, core).
Axes of the slice: x: 4, y: 4, z: 8 (z_hi: 4, z_lo: 2; z = z_hi * 2 + z_lo), core: 2. Of those that a mesh axis runs over, the one named last changes fastest.
Arguments:
- tokens: bfloat16 [1536, 8192], P('row', ('depth', 'col')), may hold values from -6 to 6
- cotangent: bfloat16 [1536, 8192], P('row', ('depth', 'col')), may hold values from -0.95703125 to 0.95703125
- gate_weight: bfloat16 [8192, 14336], P(('depth', 'col'), 'row'), may hold values from -0.0625 to 0.0625
- up_weight: bfloat16 [8192, 14336], P(('depth', 'col'), 'row'), may hold values from -0.0625 to 0.0625
- down_weight: bfloat16 [14336, 8192], P('row', ('depth', 'col')), may hold values from -0.046875 to 0.046875
Outputs:
- input_grad: bfloat16 [1536, 8192], P('row', ('depth', 'col'))
- gate_grad: bfloat16 [8192, 14336], P(('depth', 'col'), 'row')
- up_grad: bfloat16 [8192, 14336], P(('depth', 'col'), 'row')
- down_grad: bfloat16 [14336, 8192], P('row', ('depth', 'col'))
All inputs are finite; a program needn't handle non-finite values.
Results may differ from a plain program's by a relative error of at most 0.0065.
Values may be sent and summed in bfloat16 or wider, within the bound.
A program may use at most 128 MiB of HBM per device.

v0:
```python
import jax
import jax.numpy as jnp
from jax import lax
from jax.sharding import PartitionSpec as P


def sent_together(arrays, axis, dim, along):
    widths = [a.shape[along] for a in arrays]
    both = jnp.concatenate(arrays, axis=along)
    out = lax.all_gather(both, axis, axis=dim, tiled=True)
    return tuple(jnp.split(out, [sum(widths[:k]) for k in range(1, len(widths))], axis=along))


def cut_along(x, dim, count):
    before, after = (x.shape[:dim], x.shape[dim + 1 :])
    return jnp.moveaxis(x.reshape(*before, count, -1, *after), dim, 0)


def sum_at_owner(x, axis, dim):
    count = lax.axis_size(axis)
    blocks = lax.all_to_all(cut_along(x, dim, count), axis, 0, 0, tiled=True)
    return jnp.sum(blocks.astype(jnp.float32), axis=0)


def swiglu_back(gate, up, back):
    sig = jax.nn.sigmoid(gate)
    hidden = (gate * sig * up).astype(jnp.bfloat16)
    grad_gate = (back * up * sig * (1.0 + gate * (1.0 - sig))).astype(jnp.bfloat16)
    grad_up = (back * gate * sig).astype(jnp.bfloat16)
    return (hidden, grad_gate, grad_up)


def contract_rows(left, right):
    return lax.dot_general(
        left, right, (((0,), (0,)), ((), ())), preferred_element_type=jnp.float32
    )


def contract_cols(left, right):
    return lax.dot_general(
        left, right, (((1,), (1,)), ((), ())), preferred_element_type=jnp.float32
    )


def stationary(tokens, cotangent, gate_weight, up_weight, down_weight):
    rows_all, cot_all = sent_together((tokens, cotangent), "row", 0, 1)
    width = gate_weight.shape[1]
    rows_part = rows_all
    cot_part = cot_all
    gate_part = jnp.dot(rows_part, gate_weight, preferred_element_type=jnp.float32)
    up_part = jnp.dot(rows_part, up_weight, preferred_element_type=jnp.float32)
    back_part = contract_cols(cot_part, down_weight)
    summed = lax.psum_scatter(
        jnp.concatenate([gate_part, up_part, back_part], axis=1),
        ("depth", "col"),
        scatter_dimension=0,
        tiled=True,
    )
    hidden, grad_gate, grad_up = swiglu_back(
        summed[:, :width], summed[:, width : 2 * width], summed[:, 2 * width :]
    )
    hidden_piece, gate_piece, up_piece = sent_together(
        (hidden, grad_gate, grad_up), ("depth", "col"), 0, 1
    )
    rows_part = rows_all
    cot_part = cot_all
    acc_gate = contract_rows(rows_part, gate_piece)
    acc_up = contract_rows(rows_part, up_piece)
    acc_down = contract_rows(hidden_piece, cot_part)
    block = contract_cols(gate_piece, gate_weight) + contract_cols(up_piece, up_weight)
    input_grad = sum_at_owner(block.astype(jnp.bfloat16), "row", 0).astype(jnp.bfloat16)
    return (
        input_grad,
        acc_gate.astype(jnp.bfloat16),
        acc_up.astype(jnp.bfloat16),
        acc_down.astype(jnp.bfloat16),
    )


def on_device(tokens, cotangent, gate_weight, up_weight, down_weight):
    return stationary(tokens, cotangent, gate_weight, up_weight, down_weight)


def solution(mesh):
    return jax.shard_map(
        on_device,
        mesh=mesh,
        in_specs=(
            P("row", ("depth", "col")),
            P("row", ("depth", "col")),
            P(("depth", "col"), "row"),
            P(("depth", "col"), "row"),
            P("row", ("depth", "col")),
        ),
        out_specs=(
            P("row", ("depth", "col")),
            P(("depth", "col"), "row"),
            P(("depth", "col"), "row"),
            P("row", ("depth", "col")),
        ),
        check_vma=False,
    )
```

profile of v0, /device:TPU:1, one launch (start us, length us, event | category | flops | bytes accessed | tf_op | source)
XLA Modules:
  0.0 299.6 jit_solution(1222610934267227332)
XLA Ops:
  7.2 1.7 pad_maximum_fusion.2
  9.0 58.0 %all-gather.3.cloned.1.call-done = bf16[1536,1024]{1,0:T(8,128)(2,1)} async-done(((bf16[96,1024]{1,0:T(8,128)(2,1)}), bf16[1536,1024]{1,0:T(8,128)(2,1)}) %all-gather.3.cloned.1.call-update) | async-done | bytes 3145744 | tf_op jit(solution)/shard_map/all_gather | solution.py:10
  67.0 3.5 %fusion.24 = f32[1536,896]{0,1:T(8,128)S(1)} fusion(bf16[512,896]{1,0:T(8,128)(2,1)} %param.8, bf16[1536,1024]{1,0:T(8,128)(2,1)} %all-gather.3.cloned.1.call-done), kind=kOutput, calls=%fused_computation.20 | convolution fusion | flops 1409286144 | bytes 7995392 | tf_op jit(solution)/shard_map/dot_general | solution.py:51
  70.5 1.6 fusion.20
  72.2 1.7 fusion.26
  73.9 6.4 %pad_maximum_fusion = f32[1536,2688]{0,1:T(8,128)} fusion(f32[1536,896]{0,1:T(8,128)S(1)} %fusion.20, f32[1536,896]{0,1:T(8,128)S(1)} %fusion.24, f32[1536,896]{0,1:T(8,128)S(1)} %fusion.26), kind=kLoop, calls=%fused_computation | loop fusion | flops 8257536 | bytes 33030144 | tf_op jit(solution)/shard_map/concatenate | solution.py:54
  80.3 17.1 %copy.10 = f32[1536,2688]{1,0:T(8,128)} copy(f32[1536,2688]{0,1:T(8,128)} %pad_maximum_fusion) | data formatting | bytes 33030144
  97.5 97.7 %reduce-scatter.4.cloned.1.call-done = f32[96,2688]{1,0:T(8,128)} async-done(((f32[1536,2688]{1,0:T(8,128)}), f32[96,2688]{1,0:T(8,128)}) %reduce-scatter.4.cloned.1.call-update) | async-done | bytes 1032208
  195.2 1.3 fusion.28
  196.5 0.2 copy.13
  196.7 0.2 copy.12
  196.9 0.2 copy.14
  197.1 0.3 multiply_convert_fusion.2
  197.4 0.1 pad_maximum_fusion.1
  197.5 1.1 copy.9
  198.6 55.8 %all-gather.5.cloned.1.call-done = bf16[1536,2688]{1,0:T(8,128)(2,1)} async-done(((bf16[96,2688]{1,0:T(8,128)(2,1)}), bf16[1536,2688]{1,0:T(8,128)(2,1)}) %all-gather.5.cloned.1.call-update) | async-done | bytes 8257552 | tf_op jit(solution)/shard_map/all_gather | solution.py:10
  254.4 3.6 %fusion.8 = f32[1536,512]{1,0:T(8,128)S(1)} fusion(bf16[512,896]{1,0:T(8,128)(2,1)S(1)} %copy-done, bf16[1536,2688]{1,0:T(8,128)(2,1)} %all-gather.5.cloned.1.call-done), kind=kOutput, calls=%fused_computation.10 | convolution fusion | flops 1409286144 | bytes 6815744 | tf_op jit(solution)/shard_map/dot_general | solution.py:40
  258.0 4.8 %fusion = bf16[1536,512]{1,0:T(8,128)(2,1)} fusion(f32[1536,512]{1,0:T(8,128)S(1)} %fusion.8, bf16[512,896]{1,0:T(8,128)(2,1)S(1)} %copy-done.4, bf16[1536,2688]{1,0:T(8,128)(2,1)} %all-gather.5.cloned.1.call-done), kind=kOutput, calls=%fused_computation.2 | convolution fusion | flops 1410859008 | bytes 8388608 | tf_op jit(solution)/shard_map/dot_general | solution.py:40
  262.9 6.5 %all-to-all-start = ((bf16[16,96,512]{2,1,0:T(8,128)(2,1)}), bf16[16,96,512]{2,1,0:T(8,128)(2,1)S(1)}, u32[]{:S(2)}, u32[]{:S(2)}) async-start(bf16[16,96,512]{2,1,0:T(8,128)(2,1)} %bitcast.7), calls=%async_computation | async-start | bytes 3145728 | tf_op jit(solution)/shard_map/all_to_all | solution.py:21
  269.4 5.1 %fusion.10 = bf16[512,896]{1,0:T(8,128)(2,1)} fusion(bf16[1536,2688]{1,0:T(8,128)(2,1)} %all-gather.5.cloned.1.call-done, bf16[1536,1024]{1,0:T(8,128)(2,1)} %all-gather.3.cloned.1.call-done), kind=kOutput, calls=%fused_computation.12 | convolution fusion | flops 1409744896 | bytes 5242880 | tf_op jit(solution)/shard_map/dot_general | solution.py:34
  274.5 4.5 %fusion.13 = bf16[512,896]{1,0:T(8,128)(2,1)} fusion(bf16[1536,2688]{1,0:T(8,128)(2,1)} %all-gather.5.cloned.1.call-done, bf16[1536,1024]{1,0:T(8,128)(2,1)S(1)} %copy-done.2), kind=kOutput, calls=%fused_computation.13 | convolution fusion | flops 1409744896 | bytes 5242880 | tf_op jit(solution)/shard_map/dot_general | solution.py:34
  279.1 4.3 %fusion.16 = bf16[896,512]{1,0:T(8,128)(2,1)} fusion(bf16[1536,2688]{1,0:T(8,128)(2,1)} %all-gather.5.cloned.1.call-done, bf16[1536,1024]{1,0:T(8,128)(2,1)S(1)} %copy-done.2), kind=kOutput, calls=%fused_computation.14 | convolution fusion | flops 1409744896 | bytes 5242880 | tf_op jit(solution)/shard_map/dot_general | solution.py:34
  283.4 8.8 %all-to-all-done = bf16[16,96,512]{2,1,0:T(8,128)(2,1)S(1)} async-done(((bf16[16,96,512]{2,1,0:T(8,128)(2,1)}), bf16[16,96,512]{2,1,0:T(8,128)(2,1)S(1)}, u32[]{:S(2)}, u32[]{:S(2)}) %all-to-all-start) | async-done | bytes 1572896 | tf_op jit(solution)/shard_map/all_to_all | solution.py:21
  292.2 0.9 reduce_sum.12
  (16 shorter events, 0.2 us)
Async XLA Ops:
  7.2 65.0 %copy-start = (bf16[512,896]{1,0:T(8,128)(2,1)S(1)}, bf16[512,896]{1,0:T(8,128)(2,1)}, u32[]{:S(2)}) copy-start(bf16[512,896]{1,0:T(8,128)(2,1)} %param.7) | copy-start | bytes 2752516
  7.2 59.9 %all-gather.3.cloned.1.call-start = ((), (), s32[]{:S(2)}) async-start(), calls=%async_computation.2 | async-start | bytes 3342336 | tf_op jit(solution)/shard_map/all_gather | solution.py:10
  9.0 61.6 %copy-start.3 = (bf16[896,512]{1,0:T(8,128)(2,1)S(1)}, bf16[896,512]{1,0:T(8,128)(2,1)}, u32[]{:S(2)}) copy-start(bf16[896,512]{1,0:T(8,128)(2,1)} %param.9) | copy-start | bytes 2752516
  9.0 186.3 %reduce-scatter.4.cloned.1.call-start = ((), (), s32[]{:S(2)}) async-start(), calls=%async_computation.4 | async-start | bytes 17547264
  67.0 3.5 %copy-start.1 = (bf16[1536,1024]{1,0:T(8,128)(2,1)S(1)}, bf16[1536,1024]{1,0:T(8,128)(2,1)}, u32[]{:S(2)}) copy-start(bf16[1536,1024]{1,0:T(8,128)(2,1)} %all-gather.3.cloned.1.call-done) | copy-start | bytes 9437188
  97.5 156.9 %all-gather.5.cloned.1.call-start = ((), (), s32[]{:S(2)}) async-start(), calls=%async_computation.3 | async-start | bytes 8773632 | tf_op jit(solution)/shard_map/all_gather | solution.py:10
  198.6 59.4 %copy-start.4 = (bf16[512,896]{1,0:T(8,128)(2,1)S(1)}, bf16[512,896]{1,0:T(8,128)(2,1)}, u32[]{:S(2)}) copy-start(bf16[512,896]{1,0:T(8,128)(2,1)} %param.8) | copy-start | bytes 2752516
  262.9 29.3 %all-to-all-start = ((bf16[16,96,512]{2,1,0:T(8,128)(2,1)}), bf16[16,96,512]{2,1,0:T(8,128)(2,1)S(1)}, u32[]{:S(2)}, u32[]{:S(2)}) async-start(bf16[16,96,512]{2,1,0:T(8,128)(2,1)} %bitcast.7), calls=%async_computation | async-start | bytes 3145728 | tf_op jit(solution)/shard_map/all_to_all | solution.py:21
  269.4 5.1 %copy-start.2 = (bf16[1536,1024]{1,0:T(8,128)(2,1)S(1)}, bf16[1536,1024]{1,0:T(8,128)(2,1)}, u32[]{:S(2)}) copy-start(bf16[1536,1024]{1,0:T(8,128)(2,1)} %all-gather.3.cloned.1.call-done) | copy-start | bytes 9437188
Sparse Core Ops, SparseCore 0:
  11.0 55.9 all-gather.2
  97.6 97.5 reduce-scatter.3
  198.7 55.6 all-gather.4
where the time goes:
time: 300 us
  waiting for transfers between devices  220 us (73%)
  matrix products  29.3 us (10%)
  local copies, waits for them, and re-layouts  20.1 us (7%)
  between operations  13.9 us (5%)
  other arithmetic  9.43 us (3%)
  starting transfers between devices  6.66 us (2%)
    all_gather x2, waiting for transfers between devices, sent_together(): out = lax.all_gather(both, axis, axis=dim, tiled=True)  114 us
    unnamed x4, waiting for transfers between devices  97.8 us
    unnamed x14, local copies, waits for them, and re-layouts  17.7 us
    dot_general x3, matrix products, contract_rows(): lax.dot_general(left, right, (((0,), (0,)), ((), ())), preferred_element_...  14 us
    dot_general x3, matrix products, contract_cols(): lax.dot_general(left, right, (((1,), (1,)), ((), ())), preferred_element_...  10.1 us
    all_to_all x1, waiting for transfers between devices, sum_at_owner(): blocks = lax.all_to_all(cut_along(x, dim, count), axis, 0, 0, tiled=True)  8.75 us
    all_to_all x1, starting transfers between devices, sum_at_owner(): blocks = lax.all_to_all(cut_along(x, dim, count), axis, 0, 0, tiled=True)  6.53 us
    concatenate x1, other arithmetic, stationary(): jnp.concatenate([gate_part, up_part, back_part], axis=1)  6.43 us
  transfers between devices with their start and end apart: 4, of which 4 were waited for; matrix products, arithmetic and copies ran while one was open for 5% of the time, Pallas kernels for 0%

commit v1 on v0

v1 whole, which is shorter than its diff:
```python
import jax
import jax.numpy as jnp
from jax import lax
from jax.experimental import pallas as pl
from jax.experimental.pallas import tpu as pltpu
from jax.sharding import PartitionSpec as P

MESH = pl.DeviceIdType.MESH
BF16 = jnp.bfloat16
F32 = jnp.float32

STAGES = 6
ROWS = 128
CHUNK = 16
BLOCK = 48
HALF = STAGES * ROWS


def shift(dx, n):
    b = dx
    return b + b // 2 - n // 2 * (b // 3)


def kernel(
    tok, cot, wg, wu, wd,
    ig_out, gg_out, gu_out, gd_out,
    tc, tx, wgu, wdn, wgux, wdnx, q, sl, rl, ss, rs, hid, acc, accd, igb, igr,
    loc_sem, w_send, w_recv, a_send, a_recv, x_send, x_recv,
    ring_send, rl_recv, rs_recv, al_recv, as_recv, pf_send, pf_recv, ig_send, ig_recv,
):
    ff = wg.shape[1]
    depth, row, col = lax.axis_index("depth"), lax.axis_index("row"), lax.axis_index("col")
    x, y = row // 4, row % 4
    z, core = depth * 2 + col // 2, col % 2
    sign = 1 - 2 * core

    def at(xx, yy, zz, cc):
        return (zz // 2, xx * 4 + yy, (zz % 2) * 2 + cc)

    def plane(dx, dy):
        return at((x + dx) % 4, (y + dy) % 4, z, core)

    partner = at(x, y, z, 1 - core)
    far = at(x, y, (z + sign + 8) % 8, core)
    near = at(x, y, (z - sign + 8) % 8, core)

    def remote(src, dst, send, recv, device):
        return pltpu.make_async_remote_copy(
            src_ref=src, dst_ref=dst, send_sem=send, recv_sem=recv,
            device_id=device, device_id_type=MESH,
        )

    local = [
        pltpu.make_async_copy(src.at[pl.ds(BLOCK * half, BLOCK)], tc.at[t, half, pl.ds(0, BLOCK)], loc_sem.at[2 * t + half])
        for t, src in enumerate((tok, cot))
        for half in range(2)
    ]
    local += [
        pltpu.make_async_copy(wg, wgu.at[0], loc_sem.at[4]),
        pltpu.make_async_copy(wu, wgu.at[1], loc_sem.at[5]),
        pltpu.make_async_copy(wd, wdn, loc_sem.at[6]),
    ]
    for copy in local:
        copy.start()
    barrier = pltpu.get_barrier_semaphore()

    @pl.loop(1, 16)
    def _(k):
        pl.semaphore_signal(barrier, inc=1, device_id=plane(k % 4, k // 4), device_id_type=MESH)

    for device in (partner, far, near):
        pl.semaphore_signal(barrier, inc=1, device_id=device, device_id_type=MESH)
    pl.semaphore_wait(barrier, 18)

    own = pl.ds(0, BLOCK)
    east, west = plane(1, 0), plane(3, 0)
    north, south = plane(0, 1), plane(0, 3)

    def place(b, count=1):
        return pl.ds(BLOCK * b, BLOCK * count)

    a1 = [
        remote(tc.at[:, :, own], tc.at[:, :, place(2)], a_send.at[0], a_recv.at[0], east),
        remote(tc.at[:, :, own], tc.at[:, :, place(1)], a_send.at[1], a_recv.at[1], west),
        remote(tc.at[0, :, place(2)], tc.at[0, :, place(3)], a_send.at[2], a_recv.at[2], east),
        remote(tc.at[1, :, place(1)], tc.at[1, :, place(3)], a_send.at[3], a_recv.at[3], west),
        remote(tc.at[:, :, place(0, 3)], tc.at[:, :, place(12, 3)], a_send.at[4], a_recv.at[4], north),
        remote(tc.at[:, :, place(0, 3)], tc.at[:, :, place(4, 3)], a_send.at[5], a_recv.at[5], south),
        remote(tc.at[:, :, place(3)], tc.at[:, :, place(15)], a_send.at[6], a_recv.at[6], north),
        remote(tc.at[:, :, place(3)], tc.at[:, :, place(7)], a_send.at[7], a_recv.at[7], south),
        remote(tc.at[0, :, place(12, 4)], tc.at[0, :, place(8, 4)], a_send.at[8], a_recv.at[8], north),
        remote(tc.at[1, :, place(4, 4)], tc.at[1, :, place(8, 4)], a_send.at[9], a_recv.at[9], south),
    ]
    weights = [
        remote(wg, wgux.at[0], w_send.at[0], w_recv.at[0], partner),
        remote(wu, wgux.at[1], w_send.at[1], w_recv.at[1], partner),
        remote(wd, wdnx, w_send.at[2], w_recv.at[2], partner),
    ]
    for copy in local[:4]:
        copy.wait()
    a1[0].start()
    a1[1].start()
    for copy in weights:
        copy.start()
    acc[...] = jnp.zeros_like(acc)
    accd[...] = jnp.zeros_like(accd)
    for copy in local[4:]:
        copy.wait()

    def stage_rows(s):
        return pl.ds(pl.multiple_of(s * ROWS, ROWS), ROWS)

    def swap(s):
        return remote(tc.at[:, 1 - core, stage_rows(s)], tx.at[:, stage_rows(s)], x_send.at[s], x_recv.at[s], partner)

    def forward(s):
        swap(s).wait_recv()
        half = s % 2
        mine = tc[:, core, stage_rows(s), :]
        other = tx[:, stage_rows(s), :]
        for t in range(2):
            q[half, :, t * ff : (t + 1) * ff] = jnp.dot(
                mine[0], wgu[t], preferred_element_type=F32
            ) + jnp.dot(other[0], wgux[t], preferred_element_type=F32)
        dims = (((1,), (1,)), ((), ()))
        q[half, :, 2 * ff :] = lax.dot_general(
            mine[1], wdn[...], dims, preferred_element_type=F32
        ) + lax.dot_general(other[1], wdnx[...], dims, preferred_element_type=F32)

    def chunk(o):
        return pl.ds(pl.multiple_of(((o + 16) % 8) * CHUNK, CHUNK), CHUNK)

    def sum_long(s, h):
        return remote(sl.at[s, h - 1], rl.at[s, h - 1], ring_send.at[0], rl_recv.at[s, h - 1], far)

    def sum_short(s, h):
        return remote(ss.at[s, h - 1], rs.at[s, h - 1], ring_send.at[1], rs_recv.at[s, h - 1], near)

    def sum_send(s, h):
        part = q[s % 2, chunk(z + (5 - h) * sign), :]
        if h > 1:
            part = part + rl[s, h - 2].astype(F32)
        sl[s, h - 1] = part.astype(BF16)
        sum_long(s, h).start()
        if h < 4:
            part = q[s % 2, chunk(z - (4 - h) * sign), :]
            if h > 1:
                part = part + rs[s, h - 2].astype(F32)
            ss[s, h - 1] = part.astype(BF16)
            sum_short(s, h).start()

    def sum_wait(s, h):
        sum_long(s, h).wait_recv()
        if h < 4:
            sum_short(s, h).wait_recv()

    def spread_long(s, o, h):
        piece = hid.at[s, core, chunk(o)]
        return remote(piece, piece, ring_send.at[2], al_recv.at[s, h - 1], far)

    def spread_short(s, o, h):
        piece = hid.at[s, core, chunk(o)]
        return remote(piece, piece, ring_send.at[3], as_recv.at[s, h - 1], near)

    def pass_on(s, o):
        piece = hid.at[s, core, chunk(o)]
        remote(piece, piece, pf_send.at[0], pf_recv.at[s], partner).start()

    def spread_send(s, h):
        spread_long(s, z - (h - 1) * sign, h).start()
        if h < 4:
            spread_short(s, z + (h - 1) * sign, h).start()
        pass_on(s, z - (h - 1) * sign)
        if 1 < h:
            pass_on(s, z + (h - 1) * sign)

    def spread_wait(s, h):
        spread_long(s, z - h * sign, h).wait_recv()
        if h < 4:
            spread_short(s, z + h * sign, h).wait_recv()

    def pointwise(s):
        total = q[s % 2, chunk(z), :] + rl[s, 3].astype(F32) + rs[s, 2].astype(F32)
        gate, up, back = total[:, :ff], total[:, ff : 2 * ff], total[:, 2 * ff :]
        sig = jax.nn.sigmoid(gate)
        piece = chunk(z)
        hid[s, core, piece, 0:ff] = (gate * sig * up).astype(BF16)
        hid[s, core, piece, ff : 2 * ff] = (back * up * sig * (1.0 + gate * (1.0 - sig))).astype(BF16)
        hid[s, core, piece, 2 * ff :] = (back * gate * sig).astype(BF16)

    def both_halves(s):
        theirs = hid.at[s, 1 - core]
        return remote(theirs, theirs, pf_send.at[0], pf_recv.at[s], partner)

    def stage_hidden(s, t):
        return hid[s, :, :, t * ff : (t + 1) * ff].reshape(2 * ROWS, ff)

    def stage_tokens(s, t):
        return tc[t, :, stage_rows(s), :].reshape(2 * ROWS, tc.shape[-1])

    def block_copy(k):
        device = plane(shift(k % 4, 4), k // 4)
        return remote(igb.at[:, pl.ds(pl.multiple_of(k * BLOCK, BLOCK), BLOCK)], igr.at[k], ig_send.at[0], ig_recv.at[0], device)

    def input_grad(s):
        both_halves(s).wait_recv()
        dims = (((1,), (1,)), ((), ()))
        block = lax.dot_general(stage_hidden(s, 1), wgu[0], dims, preferred_element_type=F32)
        block = block + lax.dot_general(stage_hidden(s, 2), wgu[1], dims, preferred_element_type=F32)
        igb[:, stage_rows(s), :] = block.astype(BF16).reshape(2, ROWS, block.shape[-1])

        @pl.loop((ROWS * s) // BLOCK, (ROWS * (s + 1)) // BLOCK)
        def _(k):
            @pl.when(k > 0)
            def _():
                block_copy(k).start()

    outer = (((0,), (0,)), ((), ()))

    def column_grads(s):
        left = stage_tokens(s, 0)
        for t in range(2):
            acc[t] += lax.dot_general(left, stage_hidden(s, t + 1), outer, preferred_element_type=F32)

    def down_grad(s):
        accd[...] += lax.dot_general(stage_hidden(s, 0), stage_tokens(s, 1), outer, preferred_element_type=F32)

    a1[0].wait_recv()
    a1[1].wait_recv()
    swap(0).start()
    for n in (2, 3, 4, 5):
        a1[n].start()
    for copy in weights:
        copy.wait_recv()
    forward(0)
    sum_send(0, 1)

    def step(i, carry):
        summing = i < STAGES
        spreading = (i > 0) & (i <= STAGES)
        grads = i > 1

        @pl.when(grads)
        def _():
            input_grad(i - 2)

        def hop(h):
            @pl.when(summing)
            def _():
                sum_wait(i, h - 1)
                sum_send(i, h)

            @pl.when(spreading)
            def _():
                spread_wait(i - 1, h - 1)
                spread_send(i - 1, h)

        hop(2)

        @pl.when(i == 0)
        def _():
            for n in (2, 3):
                a1[n].wait_recv()
            for n in (6, 7):
                a1[n].start()

        @pl.when(i == 1)
        def _():
            for n in (4, 6, 7):
                a1[n].wait_recv()
            for n in (8, 9):
                a1[n].start()

        @pl.when(i == 2)
        def _():
            for n in (8, 9):
                a1[n].wait_recv()

        @pl.when((i > 0) & (i < STAGES - 1))
        def _():
            swap(i + 1).start()

        @pl.when(grads)
        def _():
            column_grads(i - 2)

        hop(3)

        @pl.when(i == 0)
        def _():
            a1[5].wait_recv()
            swap(1).start()

        @pl.when(i < STAGES - 1)
        def _():
            forward(i + 1)

        hop(4)

        @pl.when(i < STAGES - 1)
        def _():
            sum_send(i + 1, 1)

        @pl.when(grads)
        def _():
            down_grad(i - 2)

        @pl.when(summing)
        def _():
            sum_wait(i, 4)
            pointwise(i)
            spread_send(i, 1)

        @pl.when(spreading)
        def _():
            spread_wait(i - 1, 4)
            pass_on(i - 1, z - 4 * sign)

        return carry

    lax.fori_loop(0, STAGES + 2, step, 0)

    gg_out[...] = acc[0].astype(BF16)
    gu_out[...] = acc[1].astype(BF16)
    gd_out[...] = accd[...].astype(BF16)

    arrived = igr.at[pl.ds(1, 15)]
    remote(arrived, arrived, ig_send.at[0], ig_recv.at[0], partner).wait()
    total = igb[:, 0:BLOCK, :].astype(F32)
    for k in range(1, 16):
        total = total + igr[k].astype(F32)
    ig_out[...] = total.reshape(2 * BLOCK, total.shape[-1]).astype(BF16)

    for copy in a1 + weights:
        copy.wait_send()

    @pl.loop(0, STAGES)
    def _(s):
        swap(s).wait_send()

    remote(sl, sl, ring_send.at[0], ring_send.at[0], far).wait_send()
    remote(ss, ss, ring_send.at[1], ring_send.at[1], near).wait_send()
    remote(sl, sl, ring_send.at[2], ring_send.at[2], far).wait_send()
    remote(ss, ss, ring_send.at[3], ring_send.at[3], near).wait_send()
    mine = hid.at[:, core]
    remote(mine, mine, pf_send.at[0], pf_send.at[0], partner).wait_send()


def on_device(tokens, cotangent, gate_weight, up_weight, down_weight):
    width, ff = gate_weight.shape
    DMA = pltpu.SemaphoreType.DMA
    hbm = pl.BlockSpec(memory_space=pl.ANY)
    vmem = pl.BlockSpec(memory_space=pltpu.VMEM)
    return pl.pallas_call(
        kernel,
        out_shape=(
            jax.ShapeDtypeStruct(tokens.shape, BF16),
            jax.ShapeDtypeStruct((width, ff), BF16),
            jax.ShapeDtypeStruct((width, ff), BF16),
            jax.ShapeDtypeStruct((ff, width), BF16),
        ),
        in_specs=[hbm] * 5,
        out_specs=(vmem,) * 4,
        scratch_shapes=[
            pltpu.VMEM((2, 2, HALF, width), BF16),
            pltpu.VMEM((2, HALF, width), BF16),
            pltpu.VMEM((2, width, ff), BF16),
            pltpu.VMEM((ff, width), BF16),
            pltpu.VMEM((2, width, ff), BF16),
            pltpu.VMEM((ff, width), BF16),
            pltpu.VMEM((2, ROWS, 3 * ff), F32),
            pltpu.VMEM((STAGES, 4, CHUNK, 3 * ff), BF16),
            pltpu.VMEM((STAGES, 4, CHUNK, 3 * ff), BF16),
            pltpu.VMEM((STAGES, 3, CHUNK, 3 * ff), BF16),
            pltpu.VMEM((STAGES, 3, CHUNK, 3 * ff), BF16),
            pltpu.VMEM((STAGES, 2, ROWS, 3 * ff), BF16),
            pltpu.VMEM((2, width, ff), F32),
            pltpu.VMEM((ff, width), F32),
            pltpu.VMEM((2, HALF, width), BF16),
            pltpu.VMEM((16, 2, BLOCK, width), BF16),
            DMA((7,)),
            DMA((3,)),
            DMA((3,)),
            DMA((10,)),
            DMA((10,)),
            DMA((STAGES,)),
            DMA((STAGES,)),
            DMA((4,)),
            DMA((STAGES, 4)),
            DMA((STAGES, 3)),
            DMA((STAGES, 4)),
            DMA((STAGES, 3)),
            DMA((1,)),
            DMA((STAGES,)),
            DMA((1,)),
            DMA((1,)),
        ],
        compiler_params=pltpu.CompilerParams(
            collective_id=0, has_side_effects=True, vmem_limit_bytes=60 * 1024 * 1024
        ),
    )(tokens, cotangent, gate_weight, up_weight, down_weight)


def solution(mesh):
    return jax.shard_map(
        on_device,
        mesh=mesh,
        in_specs=(
            P("row", ("depth", "col")),
            P("row", ("depth", "col")),
            P(("depth", "col"), "row"),
            P(("depth", "col"), "row"),
            P("row", ("depth", "col")),
        ),
        out_specs=(
            P("row", ("depth", "col")),
            P(("depth", "col"), "row"),
            P(("depth", "col"), "row"),
            P("row", ("depth", "col")),
        ),
        check_vma=False,
    )
```

time: 300 us -> 156 us (0.52)
  waiting for transfers between devices: 220 us -> 0 us
  Pallas kernels: 0 us -> 149 us
  matrix products: 29.3 us -> 0 us
  local copies, waits for them, and re-layouts: 20.1 us -> 6.23 us
  between operations: 13.9 us -> 0.64 us
  other arithmetic: 9.43 us -> 0 us
  starting transfers between devices: 6.66 us -> 0 us
    pallas_call x0 -> x1, Pallas kernels: none -> 149 us  [on_device(): pl.pallas_call(kernel, out_shape=(jax.ShapeDtypeStruct(tokens.shape, BF16...]
    all_gather x2 -> x0, waiting for transfers between devices: 114 us -> none  [sent_together(): out = lax.all_gather(both, axis, axis=dim, tiled=True)]
    unnamed x4 -> x0, waiting for transfers between devices: 97.8 us -> none
    dot_general x8 -> x0, matrix products: 29.3 us -> none  [the longest x3 14 us: contract_rows(): lax.dot_general(left, right, (((0,), (0,)), ((), ())), preferred_element_...]
    unnamed x14 -> x8, local copies, waits for them, and re-layouts: 17.7 us -> 6.23 us
    all_to_all x1 -> x0, waiting for transfers between devices: 8.75 us -> none  [sum_at_owner(): blocks = lax.all_to_all(cut_along(x, dim, count), axis, 0, 0, tiled=True)]
    concatenate x3 -> x0, other arithmetic: 8.28 us -> none  [the longest x1 6.43 us: stationary(): jnp.concatenate([gate_part, up_part, back_part], axis=1)]
    all_to_all x1 -> x0, starting transfers between devices: 6.53 us -> none  [sum_at_owner(): blocks = lax.all_to_all(cut_along(x, dim, count), axis, 0, 0, tiled=True)]
  transfers between devices with their start and end apart: 4 -> 0, of which waited for: 4 -> 0; matrix products, arithmetic and copies ran while one was open for 5% -> 0% of each run, Pallas kernels for 0% -> 0%
where the time goes in v1:
time: 156 us
  Pallas kernels  149 us (96%)
  local copies, waits for them, and re-layouts  6.23 us (4%)
    pallas_call x1, Pallas kernels, on_device(): pl.pallas_call(kernel, out_shape=(jax.ShapeDtypeStruct(tokens.shape, BF16...  149 us
    unnamed x8, local copies, waits for them, and re-layouts  6.23 us

profile of v1, /device:TPU:1, one launch (start us, length us, event | category | flops | bytes accessed | tf_op | source)
XLA Modules:
  0.0 156.0 jit_solution(11177353674854137619)
XLA Ops:
  0.6 149.1 %shard_map.84 = (bf16[96,512]{1,0:T(8,128)(2,1)}, bf16[512,896]{1,0:T(8,128)(2,1)}, bf16[512,896]{1,0:T(8,128)(2,1)}, bf16[896,512]{1,0:T(8,128)(2,1)}) custom-call(bf16[96,512]{1,0:T(8,128)(2,1)} %tok.1, bf16[96,512]{1,0:T(8,128)(2,1)} %cot.1, bf16[512,896]{1,0:T(8,128)(2,1)} %wg.1, bf16[512,896]{1,0:T(8,128)(2,1)} %wu.1, bf16[896,512]{1,0:T(8,128)(2,1)} %wd.1), custom_call_target="tpu_custom_call" | custom-call | tf_op jit(solution)/shard_map/pallas_call | solution.py:354
  149.7 1.5 copy.13
  151.3 0.0 copy-start.1
  151.3 2.3 %copy.14 = bf16[512,896]{1,0:T(8,128)(2,1)} copy(bf16[512,896]{1,0:T(8,128)(2,1)} %get-tuple-element.9) | data formatting | bytes 1835008
  153.5 0.0 copy-done.1
  153.5 0.0 copy-start
  153.5 0.9 copy.15
  154.4 0.6 copy-done
  155.0 0.9 copy.16
Async XLA Ops:
  151.3 2.3 %copy-start.1 = (bf16[512,896]{1,0:T(8,128)(2,1)S(1)}, bf16[512,896]{1,0:T(8,128)(2,1)}, u32[]{:S(2)}) copy-start(bf16[512,896]{1,0:T(8,128)(2,1)} %get-tuple-element.10) | copy-start | bytes 2752516
  153.5 1.5 copy-start

commit v2 on v1

v2 whole, which is shorter than its diff:
```python
import jax
import jax.numpy as jnp
from jax import lax
from jax.experimental import pallas as pl
from jax.experimental.pallas import tpu as pltpu
from jax.sharding import PartitionSpec as P

MESH = pl.DeviceIdType.MESH
BF16 = jnp.bfloat16
F32 = jnp.float32

STAGES = 6
ROWS = 128
CHUNK = 16
BLOCK = 48
HALF = STAGES * ROWS
PARTS = ((0, 1280), (1280, 1408))


PLACES = (
    (0, 0), (1, 0), (0, 1), (2, 0), (3, 1), (3, 3), (1, 3), (2, 1),
    (2, 3), (0, 2), (1, 2), (3, 2), (2, 2), (1, 1), (3, 0), (0, 3),
)


def kernel(
    tok, cot, wg, wu, wd,
    ig_out, gg_out, gu_out, gd_out,
    tc, tx, wgu, wdn, wgux, wdnx, q, sl, rl, ss, rs, hid, igb, igr,
    loc_sem, w_send, w_recv, a_send, a_recv, x_send, x_recv,
    ring_send, rl_recv, rs_recv, al_recv, as_recv, pf_send, pf_recv, ig_send, ig_recv,
):
    ff = wg.shape[1]
    depth, row, col = lax.axis_index("depth"), lax.axis_index("row"), lax.axis_index("col")
    x, y = row // 4, row % 4
    z, core = depth * 2 + col // 2, col % 2
    sign = 1 - 2 * core

    def at(xx, yy, zz, cc):
        return (zz // 2, xx * 4 + yy, (zz % 2) * 2 + cc)

    def plane(dx, dy):
        return at((x + dx) % 4, (y + dy) % 4, z, core)

    partner = at(x, y, z, 1 - core)
    far = at(x, y, (z + sign + 8) % 8, core)
    near = at(x, y, (z - sign + 8) % 8, core)

    def remote(src, dst, send, recv, device):
        return pltpu.make_async_remote_copy(
            src_ref=src, dst_ref=dst, send_sem=send, recv_sem=recv,
            device_id=device, device_id_type=MESH,
        )

    local = [
        pltpu.make_async_copy(src.at[pl.ds(BLOCK * half, BLOCK)], tc.at[t, half, pl.ds(0, BLOCK)], loc_sem.at[2 * t + half])
        for t, src in enumerate((tok, cot))
        for half in range(2)
    ]
    local += [
        pltpu.make_async_copy(wg, wgu.at[0], loc_sem.at[4]),
        pltpu.make_async_copy(wu, wgu.at[1], loc_sem.at[5]),
        pltpu.make_async_copy(wd, wdn, loc_sem.at[6]),
    ]
    for copy in local:
        copy.start()
    barrier = pltpu.get_barrier_semaphore()

    @pl.loop(1, 16)
    def _(k):
        pl.semaphore_signal(barrier, inc=1, device_id=plane(k % 4, k // 4), device_id_type=MESH)

    for device in (partner, far, near):
        pl.semaphore_signal(barrier, inc=1, device_id=device, device_id_type=MESH)
    pl.semaphore_wait(barrier, 18)

    east, west = plane(1, 0), plane(3, 0)
    north, south = plane(0, 1), plane(0, 3)

    def block(t, k):
        rows = pl.ds(BLOCK * k, BLOCK)
        return tc.at[:, :, rows] if t is None else tc.at[t, :, rows]

    hops = (
        (None, 0, 14, east), (None, 0, 1, west), (None, 0, 15, north), (None, 0, 2, south),
        (0, 14, 3, east), (1, 1, 3, west),
        (None, 1, 6, north), (None, 14, 5, north), (None, 14, 4, south), (None, 1, 13, south),
        (0, 15, 9, north), (1, 2, 9, south),
        (None, 3, 8, north), (None, 3, 7, south),
        (0, 6, 10, north), (1, 13, 10, south), (0, 5, 11, north), (1, 4, 11, south),
        (0, 8, 12, north), (1, 7, 12, south),
    )
    a1 = [
        remote(block(t, src), block(t, dst), a_send.at[n], a_recv.at[n], device)
        for n, (t, src, dst, device) in enumerate(hops)
    ]

    def tokens_in(*numbers):
        for n in numbers:
            a1[n].wait_recv()

    def tokens_out(*numbers):
        for n in numbers:
            a1[n].start()

    weights = [
        remote(wg, wgux.at[0], w_send.at[0], w_recv.at[0], partner),
        remote(wu, wgux.at[1], w_send.at[1], w_recv.at[1], partner),
        remote(wd, wdnx, w_send.at[2], w_recv.at[2], partner),
    ]
    for copy in local[:4]:
        copy.wait()
    tokens_out(0, 1, 2, 3)
    for copy in weights:
        copy.start()
    for out in (gg_out, gu_out, gd_out):
        out[...] = jnp.zeros_like(out)
    for copy in local[4:]:
        copy.wait()

    def stage_rows(s):
        return pl.ds(pl.multiple_of(s * ROWS, ROWS), ROWS)

    def swap(s):
        return remote(tc.at[:, 1 - core, stage_rows(s)], tx.at[:, stage_rows(s)], x_send.at[s], x_recv.at[s], partner)

    def forward(s):
        swap(s).wait_recv()
        slot = s % 3
        mine = tc[:, core, stage_rows(s), :]
        other = tx[:, stage_rows(s), :]
        for t in range(2):
            q[slot, :, t * ff : (t + 1) * ff] = jnp.dot(
                mine[0], wgu[t], preferred_element_type=F32
            ) + jnp.dot(other[0], wgux[t], preferred_element_type=F32)
        dims = (((1,), (1,)), ((), ()))
        q[slot, :, 2 * ff :] = lax.dot_general(
            mine[1], wdn[...], dims, preferred_element_type=F32
        ) + lax.dot_general(other[1], wdnx[...], dims, preferred_element_type=F32)

    def chunk(o):
        return pl.ds(pl.multiple_of(((o + 16) % 8) * CHUNK, CHUNK), CHUNK)

    def part_of(ref, p):
        return ref.at[:, pl.ds(*PARTS[p])]

    def sum_long(s, h, p):
        return remote(
            part_of(sl.at[s, h - 1], p), part_of(rl.at[s, h - 1], p), ring_send.at[0], rl_recv.at[s, h - 1, p], far
        )

    def sum_short(s, h, p):
        return remote(
            part_of(ss.at[s, h - 1], p), part_of(rs.at[s, h - 1], p), ring_send.at[1], rs_recv.at[s, h - 1, p], near
        )

    def sum_send(s, h, p):
        cols = pl.ds(*PARTS[p])
        part = q[s % 3, chunk(z + (5 - h) * sign), cols]
        if h > 1:
            part = part + rl[s, h - 2, :, cols].astype(F32)
        sl[s, h - 1, :, cols] = part.astype(BF16)
        sum_long(s, h, p).start()
        if h < 4:
            part = q[s % 3, chunk(z - (4 - h) * sign), cols]
            if h > 1:
                part = part + rs[s, h - 2, :, cols].astype(F32)
            ss[s, h - 1, :, cols] = part.astype(BF16)
            sum_short(s, h, p).start()

    def sum_wait(s, h, p):
        sum_long(s, h, p).wait_recv()
        if h < 4:
            sum_short(s, h, p).wait_recv()

    def sum_on(s, h):
        for p in range(2):
            sum_wait(s, h, p)
            sum_send(s, h + 1, p)

    def piece_of(s, o):
        return hid.at[s, core, chunk(o)]

    def spread_long(s, o, h, p):
        piece = part_of(piece_of(s, o), p)
        return remote(piece, piece, ring_send.at[2], al_recv.at[s, h - 1, p], far)

    def spread_short(s, o, h, p):
        piece = part_of(piece_of(s, o), p)
        return remote(piece, piece, ring_send.at[3], as_recv.at[s, h - 1, p], near)

    def pass_on(s, o):
        piece = piece_of(s, o)
        remote(piece, piece, pf_send.at[0], pf_recv.at[s], partner).start()

    def spread_send(s, h, p):
        spread_long(s, z - (h - 1) * sign, h, p).start()
        if h < 4:
            spread_short(s, z + (h - 1) * sign, h, p).start()

    def spread_wait(s, h, p):
        spread_long(s, z - h * sign, h, p).wait_recv()
        if h < 4:
            spread_short(s, z + h * sign, h, p).wait_recv()

    def spread_on(s, h):
        for p in range(2):
            spread_wait(s, h, p)
            if h < 4:
                spread_send(s, h + 1, p)
        pass_on(s, z - h * sign)
        if h < 4:
            pass_on(s, z + h * sign)

    def pointwise(s):
        total = q[s % 3, chunk(z), :] + rl[s, 3].astype(F32) + rs[s, 2].astype(F32)
        gate, up, back = total[:, :ff], total[:, ff : 2 * ff], total[:, 2 * ff :]
        sig = jax.nn.sigmoid(gate)
        piece = chunk(z)
        hid[s, core, piece, 0:ff] = (gate * sig * up).astype(BF16)
        hid[s, core, piece, ff : 2 * ff] = (back * up * sig * (1.0 + gate * (1.0 - sig))).astype(BF16)
        hid[s, core, piece, 2 * ff :] = (back * gate * sig).astype(BF16)

    def both_halves(s):
        theirs = hid.at[s, 1 - core]
        return remote(theirs, theirs, pf_send.at[0], pf_recv.at[s], partner)

    def stage_hidden(s, t):
        return hid[s, :, :, t * ff : (t + 1) * ff].reshape(2 * ROWS, ff)

    def stage_tokens(s, t):
        return tc[t, :, stage_rows(s), :].reshape(2 * ROWS, tc.shape[-1])

    def block_copy(k):
        return remote(igb.at[:, pl.ds(BLOCK * k, BLOCK)], igr.at[k], ig_send.at[0], ig_recv.at[0], plane(*PLACES[k]))

    def input_grad(s):
        both_halves(s).wait_recv()
        dims = (((1,), (1,)), ((), ()))
        block = lax.dot_general(stage_hidden(s, 1), wgu[0], dims, preferred_element_type=F32)
        block = block + lax.dot_general(stage_hidden(s, 2), wgu[1], dims, preferred_element_type=F32)
        igb[:, stage_rows(s), :] = block.astype(BF16).reshape(2, ROWS, block.shape[-1])

        for stage in range(STAGES):

            @pl.when(s == stage)
            def _():
                for k in range(max(1, ROWS * stage // BLOCK), ROWS * (stage + 1) // BLOCK):
                    block_copy(k).start()

    outer = (((0,), (0,)), ((), ()))

    def column_grads(s):
        left = stage_tokens(s, 0)
        for t, out in enumerate((gg_out, gu_out)):
            out[...] += lax.dot_general(left, stage_hidden(s, t + 1), outer, preferred_element_type=F32)

    def down_grad(s):
        gd_out[...] += lax.dot_general(stage_hidden(s, 0), stage_tokens(s, 1), outer, preferred_element_type=F32)

    tokens_in(0, 1, 2, 3)
    swap(0).start()
    tokens_out(4, 5, 7, 8, 6)
    for copy in weights:
        copy.wait_recv()
    forward(0)
    sum_send(0, 1, 0)
    sum_send(0, 1, 1)

    def step(i, carry):
        front = i < STAGES
        back = (i > 0) & (i < STAGES + 1)
        out_front = (i > 1) & (i < STAGES + 2)
        out_back = (i > 2) & (i < STAGES + 3)
        grads = i > 3
        more = i < STAGES - 1

        @pl.when(back)
        def _():
            sum_on(i - 1, 2)

        @pl.when(out_back)
        def _():
            spread_on(i - 3, 2)

        @pl.when(grads)
        def _():
            input_grad(i - 4)

        @pl.when(front)
        def _():
            sum_on(i, 1)

        @pl.when(out_front)
        def _():
            spread_on(i - 2, 1)

        @pl.when(back)
        def _():
            sum_on(i - 1, 3)

        @pl.when(out_back)
        def _():
            spread_on(i - 3, 3)

        @pl.when(i == 0)
        def _():
            tokens_in(4, 5)
            tokens_out(12, 13, 9, 10, 11)
            tokens_in(7, 8)

        @pl.when(i == 1)
        def _():
            tokens_in(6, 9)
            tokens_out(14, 15, 16, 17)
            tokens_in(12, 13)
            tokens_out(18, 19)

        @pl.when(i == 2)
        def _():
            tokens_in(10, 11, 14, 15)

        @pl.when(i == 3)
        def _():
            tokens_in(16, 17, 18, 19)

        @pl.when(more)
        def _():
            swap(i + 1).start()

        @pl.when(grads)
        def _():
            column_grads(i - 4)

        @pl.when(more)
        def _():
            forward(i + 1)
            sum_send(i + 1, 1, 0)
            sum_send(i + 1, 1, 1)

        @pl.when(back)
        def _():
            sum_wait(i - 1, 4, 0)
            sum_wait(i - 1, 4, 1)
            pointwise(i - 1)
            spread_send(i - 1, 1, 0)
            spread_send(i - 1, 1, 1)
            pass_on(i - 1, z)

        @pl.when(out_back)
        def _():
            spread_on(i - 3, 4)

        @pl.when(grads)
        def _():
            down_grad(i - 4)

        return carry

    lax.fori_loop(0, STAGES + 4, step, 0)

    arrived = igr.at[pl.ds(1, 15)]
    remote(arrived, arrived, ig_send.at[0], ig_recv.at[0], partner).wait()
    total = igb[:, 0:BLOCK, :].astype(F32)
    for k in range(1, 16):
        total = total + igr[k].astype(F32)
    ig_out[...] = total.reshape(2 * BLOCK, total.shape[-1])

    for copy in a1 + weights:
        copy.wait_send()

    @pl.loop(0, STAGES)
    def _(s):
        swap(s).wait_send()

    remote(sl, sl, ring_send.at[0], ring_send.at[0], far).wait_send()
    remote(ss, ss, ring_send.at[1], ring_send.at[1], near).wait_send()
    remote(sl, sl, ring_send.at[2], ring_send.at[2], far).wait_send()
    remote(ss, ss, ring_send.at[3], ring_send.at[3], near).wait_send()
    mine = hid.at[:, core]
    remote(mine, mine, pf_send.at[0], pf_send.at[0], partner).wait_send()


def rounded(*refs):
    wide, out, narrow, sems = refs[:4], refs[4:8], refs[8:12], refs[12]
    copies = [pltpu.make_async_copy(b, o, sems.at[n]) for n, (b, o) in enumerate(zip(narrow, out))]
    for a, b, copy in zip(wide, narrow, copies):
        b[...] = a[...].astype(BF16)
        copy.start()
    for copy in copies:
        copy.wait()


def on_device(tokens, cotangent, gate_weight, up_weight, down_weight):
    width, ff = gate_weight.shape
    DMA = pltpu.SemaphoreType.DMA
    hbm = pl.BlockSpec(memory_space=pltpu.HBM)
    vmem = pl.BlockSpec(memory_space=pltpu.VMEM)
    outs = pl.pallas_call(
        kernel,
        out_shape=(
            pltpu.VMEM(tokens.shape, F32),
            pltpu.VMEM((width, ff), F32),
            pltpu.VMEM((width, ff), F32),
            pltpu.VMEM((ff, width), F32),
        ),
        in_specs=[hbm] * 5,
        out_specs=(vmem,) * 4,
        scratch_shapes=[
            pltpu.VMEM((2, 2, HALF, width), BF16),
            pltpu.VMEM((2, HALF, width), BF16),
            pltpu.VMEM((2, width, ff), BF16),
            pltpu.VMEM((ff, width), BF16),
            pltpu.VMEM((2, width, ff), BF16),
            pltpu.VMEM((ff, width), BF16),
            pltpu.VMEM((3, ROWS, 3 * ff), F32),
            pltpu.VMEM((STAGES, 4, CHUNK, 3 * ff), BF16),
            pltpu.VMEM((STAGES, 4, CHUNK, 3 * ff), BF16),
            pltpu.VMEM((STAGES, 3, CHUNK, 3 * ff), BF16),
            pltpu.VMEM((STAGES, 3, CHUNK, 3 * ff), BF16),
            pltpu.VMEM((STAGES, 2, ROWS, 3 * ff), BF16),
            pltpu.VMEM((2, HALF, width), BF16),
            pltpu.VMEM((16, 2, BLOCK, width), BF16),
            DMA((7,)),
            DMA((3,)),
            DMA((3,)),
            DMA((20,)),
            DMA((20,)),
            DMA((STAGES,)),
            DMA((STAGES,)),
            DMA((4,)),
            DMA((STAGES, 4, 2)),
            DMA((STAGES, 3, 2)),
            DMA((STAGES, 4, 2)),
            DMA((STAGES, 3, 2)),
            DMA((1,)),
            DMA((STAGES,)),
            DMA((1,)),
            DMA((1,)),
        ],
        compiler_params=pltpu.CompilerParams(
            collective_id=0, has_side_effects=True, vmem_limit_bytes=61300000
        ),
    )(tokens, cotangent, gate_weight, up_weight, down_weight)
    outs = [pltpu.with_memory_space_constraint(out, pltpu.VMEM) for out in outs]
    return pl.pallas_call(
        rounded,
        out_shape=tuple(jax.ShapeDtypeStruct(out.shape, BF16) for out in outs),
        in_specs=[vmem] * 4,
        out_specs=(hbm,) * 4,
        scratch_shapes=[pltpu.VMEM(out.shape, BF16) for out in outs] + [DMA((4,))],
        compiler_params=pltpu.CompilerParams(vmem_limit_bytes=16 * 1024 * 1024),
    )(*outs)


def solution(mesh):
    return jax.shard_map(
        on_device,
        mesh=mesh,
        in_specs=(
            P("row", ("depth", "col")),
            P("row", ("depth", "col")),
            P(("depth", "col"), "row"),
            P(("depth", "col"), "row"),
            P("row", ("depth", "col")),
        ),
        out_specs=(
            P("row", ("depth", "col")),
            P(("depth", "col"), "row"),
            P(("depth", "col"), "row"),
            P("row", ("depth", "col")),
        ),
        check_vma=False,
    )
```

time: 156 us -> 130 us (0.83)
  Pallas kernels: 149 us -> 130 us
  local copies, waits for them, and re-layouts: 6.23 us -> 0 us
    pallas_call x1 -> x2, Pallas kernels: 149 us -> 130 us  [the longest x1 128 us: on_device(): pl.pallas_call(kernel, out_shape=(pltpu.VMEM(tokens.shape, F32), pltpu.VM...]
    unnamed x8 -> x0, local copies, waits for them, and re-layouts: 6.23 us -> none
where the time goes in v2:
time: 130 us
  Pallas kernels  130 us (100%)
    pallas_call x1, Pallas kernels, on_device(): pl.pallas_call(kernel, out_shape=(pltpu.VMEM(tokens.shape, F32), pltpu.VM...  128 us

profile of v2, /device:TPU:1, one launch (start us, length us, event | category | flops | bytes accessed | tf_op | source)
XLA Modules:
  0.0 130.4 jit_solution(648971151094472286)
XLA Ops:
  0.6 128.1 %shard_map.84 = (f32[96,512]{1,0:T(8,128)S(1)}, f32[512,896]{1,0:T(8,128)S(1)}, f32[512,896]{1,0:T(8,128)S(1)}, f32[896,512]{1,0:T(8,128)S(1)}) custom-call(bf16[96,512]{1,0:T(8,128)(2,1)} %tok.1, bf16[96,512]{1,0:T(8,128)(2,1)} %cot.1, bf16[512,896]{1,0:T(8,128)(2,1)} %wg.1, bf16[512,896]{1,0:T(8,128)(2,1)} %wu.1, bf16[896,512]{1,0:T(8,128)(2,1)} %wd.1), custom_call_target="tpu_custom_call" | custom-call | tf_op jit(solution)/shard_map/pallas_call | solution.py:399
  128.7 1.7 %shard_map.85 = (bf16[96,512]{1,0:T(8,128)(2,1)}, bf16[512,896]{1,0:T(8,128)(2,1)}, bf16[512,896]{1,0:T(8,128)(2,1)}, bf16[896,512]{1,0:T(8,128)(2,1)}) custom-call(f32[96,512]{1,0:T(8,128)S(1)} %get-tuple-element.8.refs_0_, f32[512,896]{1,0:T(8,128)S(1)} %get-tuple-element.9.refs_1_, f32[512,896]{1,0:T(8,128)S(1)} %get-tuple-element.10.refs_2_, ...), custom_call_target="tpu_custom_call" | custom-call | tf_op jit(solution)/shard_map/pallas_call | solution.py:446

commit v3 on v2

--- a/solution.py
+++ b/solution.py
@@ -66,13 +66,10 @@
         copy.start()
     barrier = pltpu.get_barrier_semaphore()
 
-    @pl.loop(1, 16)
-    def _(k):
-        pl.semaphore_signal(barrier, inc=1, device_id=plane(k % 4, k // 4), device_id_type=MESH)
-
-    for device in (partner, far, near):
+    neighbours = (partner, far, near, plane(1, 0), plane(3, 0), plane(0, 1), plane(0, 3))
+    for device in neighbours:
         pl.semaphore_signal(barrier, inc=1, device_id=device, device_id_type=MESH)
-    pl.semaphore_wait(barrier, 18)
+    pl.semaphore_wait(barrier, len(neighbours))
 
     east, west = plane(1, 0), plane(3, 0)
     north, south = plane(0, 1), plane(0, 3)
@@ -124,19 +121,21 @@
     def swap(s):
         return remote(tc.at[:, 1 - core, stage_rows(s)], tx.at[:, stage_rows(s)], x_send.at[s], x_recv.at[s], partner)
 
-    def forward(s):
-        swap(s).wait_recv()
+    def forward_in(s):
         slot = s % 3
-        mine = tc[:, core, stage_rows(s), :]
-        other = tx[:, stage_rows(s), :]
+        mine, other = tc[0, core, stage_rows(s), :], tx[0, stage_rows(s), :]
         for t in range(2):
             q[slot, :, t * ff : (t + 1) * ff] = jnp.dot(
-                mine[0], wgu[t], preferred_element_type=F32
-            ) + jnp.dot(other[0], wgux[t], preferred_element_type=F32)
+                mine, wgu[t], preferred_element_type=F32
+            ) + jnp.dot(other, wgux[t], preferred_element_type=F32)
+
+    def forward_out(s):
+        slot = s % 3
+        mine, other = tc[1, core, stage_rows(s), :], tx[1, stage_rows(s), :]
         dims = (((1,), (1,)), ((), ()))
         q[slot, :, 2 * ff :] = lax.dot_general(
-            mine[1], wdn[...], dims, preferred_element_type=F32
-        ) + lax.dot_general(other[1], wdnx[...], dims, preferred_element_type=F32)
+            mine, wdn[...], dims, preferred_element_type=F32
+        ) + lax.dot_general(other, wdnx[...], dims, preferred_element_type=F32)
 
     def chunk(o):
         return pl.ds(pl.multiple_of(((o + 16) % 8) * CHUNK, CHUNK), CHUNK)
@@ -260,11 +259,14 @@
 
     tokens_in(0, 1, 2, 3)
     swap(0).start()
-    tokens_out(4, 5, 7, 8, 6)
-    for copy in weights:
+    tokens_out(4, 5, 7, 8, 6, 9)
+    for copy in weights[:2]:
         copy.wait_recv()
-    forward(0)
+    swap(0).wait_recv()
+    forward_in(0)
     sum_send(0, 1, 0)
+    weights[2].wait_recv()
+    forward_out(0)
     sum_send(0, 1, 1)
 
     def step(i, carry):
@@ -275,6 +277,13 @@
         grads = i > 3
         more = i < STAGES - 1
 
+        @pl.when(i == 0)
+        def _():
+            tokens_in(4, 5)
+            tokens_out(12, 13, 10, 11)
+            tokens_in(7, 8)
+            swap(1).start()
+
         @pl.when(back)
         def _():
             sum_on(i - 1, 2)
@@ -294,20 +303,6 @@
         @pl.when(out_front)
         def _():
             spread_on(i - 2, 1)
-
-        @pl.when(back)
-        def _():
-            sum_on(i - 1, 3)
-
-        @pl.when(out_back)
-        def _():
-            spread_on(i - 3, 3)
-
-        @pl.when(i == 0)
-        def _():
-            tokens_in(4, 5)
-            tokens_out(12, 13, 9, 10, 11)
-            tokens_in(7, 8)
 
         @pl.when(i == 1)
         def _():
@@ -324,18 +319,28 @@
         def _():
             tokens_in(16, 17, 18, 19)
 
+        @pl.when((i > 0) & more)
+        def _():
+            swap(i + 1).start()
+
+        @pl.when(back)
+        def _():
+            sum_on(i - 1, 3)
+
+        @pl.when(out_back)
+        def _():
+            spread_on(i - 3, 3)
+
+        @pl.when(grads)
+        def _():
+            column_grads(i - 4)
+
         @pl.when(more)
         def _():
-            swap(i + 1).start()
-
-        @pl.when(grads)
-        def _():
-            column_grads(i - 4)
-
-        @pl.when(more)
-        def _():
-            forward(i + 1)
+            swap(i + 1).wait_recv()
+            forward_in(i + 1)
             sum_send(i + 1, 1, 0)
+            forward_out(i + 1)
             sum_send(i + 1, 1, 1)
 
         @pl.when(back)

time: 130 us -> 125 us (0.962)
  Pallas kernels: 130 us -> 124 us
    pallas_call x1, Pallas kernels: 128 us -> 123 us  [on_device(): pl.pallas_call(kernel, out_shape=(pltpu.VMEM(tokens.shape, F32), pltpu.VM...]
where the time goes in v3:
time: 125 us
  Pallas kernels  124 us (99%)
    pallas_call x1, Pallas kernels, on_device(): pl.pallas_call(kernel, out_shape=(pltpu.VMEM(tokens.shape, F32), pltpu.VM...  123 us

profile of v3, /device:TPU:1, one launch (start us, length us, event | category | flops | bytes accessed | tf_op | source)
XLA Modules:
  0.0 125.1 jit_solution(13347040756665578993)
XLA Ops:
  0.6 122.8 %shard_map.84 = (f32[96,512]{1,0:T(8,128)S(1)}, f32[512,896]{1,0:T(8,128)S(1)}, f32[512,896]{1,0:T(8,128)S(1)}, f32[896,512]{1,0:T(8,128)S(1)}) custom-call(bf16[96,512]{1,0:T(8,128)(2,1)} %tok.1, bf16[96,512]{1,0:T(8,128)(2,1)} %cot.1, bf16[512,896]{1,0:T(8,128)(2,1)} %wg.1, bf16[512,896]{1,0:T(8,128)(2,1)} %wu.1, bf16[896,512]{1,0:T(8,128)(2,1)} %wd.1), custom_call_target="tpu_custom_call" | custom-call | tf_op jit(solution)/shard_map/pallas_call | solution.py:404
  123.5 1.7 %shard_map.85 = (bf16[96,512]{1,0:T(8,128)(2,1)}, bf16[512,896]{1,0:T(8,128)(2,1)}, bf16[512,896]{1,0:T(8,128)(2,1)}, bf16[896,512]{1,0:T(8,128)(2,1)}) custom-call(f32[96,512]{1,0:T(8,128)S(1)} %get-tuple-element.8.refs_0_, f32[512,896]{1,0:T(8,128)S(1)} %get-tuple-element.9.refs_1_, f32[512,896]{1,0:T(8,128)S(1)} %get-tuple-element.10.refs_2_, ...), custom_call_target="tpu_custom_call" | custom-call | tf_op jit(solution)/shard_map/pallas_call | solution.py:451

commit v4 on v3

--- a/solution.py
+++ b/solution.py
@@ -14,6 +14,7 @@
 CHUNK = 16
 BLOCK = 48
 HALF = STAGES * ROWS
+LATE = (STAGES - 1) * ROWS // BLOCK
 PARTS = ((0, 1280), (1280, 1408))
 
 
@@ -26,7 +27,7 @@
 def kernel(
     tok, cot, wg, wu, wd,
     ig_out, gg_out, gu_out, gd_out,
-    tc, tx, wgu, wdn, wgux, wdnx, q, sl, rl, ss, rs, hid, igb, igr,
+    tc, tx, wgu, wdn, wgux, wdnx, q, sl, rl, ss, rs, hid, accg, accu, accd, igb, igr,
     loc_sem, w_send, w_recv, a_send, a_recv, x_send, x_recv,
     ring_send, rl_recv, rs_recv, al_recv, as_recv, pf_send, pf_recv, ig_send, ig_recv,
 ):
@@ -79,13 +80,14 @@
         return tc.at[:, :, rows] if t is None else tc.at[t, :, rows]
 
     hops = (
-        (None, 0, 14, east), (None, 0, 1, west), (None, 0, 15, north), (None, 0, 2, south),
+        (0, 0, 14, east), (0, 0, 1, west), (0, 0, 15, north), (0, 0, 2, south),
         (0, 14, 3, east), (1, 1, 3, west),
         (None, 1, 6, north), (None, 14, 5, north), (None, 14, 4, south), (None, 1, 13, south),
         (0, 15, 9, north), (1, 2, 9, south),
         (None, 3, 8, north), (None, 3, 7, south),
         (0, 6, 10, north), (1, 13, 10, south), (0, 5, 11, north), (1, 4, 11, south),
         (0, 8, 12, north), (1, 7, 12, south),
+        (1, 0, 14, east), (1, 0, 1, west), (1, 0, 15, north), (1, 0, 2, south),
     )
     a1 = [
         remote(block(t, src), block(t, dst), a_send.at[n], a_recv.at[n], device)
@@ -107,21 +109,24 @@
     ]
     for copy in local[:4]:
         copy.wait()
-    tokens_out(0, 1, 2, 3)
+    tokens_out(0, 1, 2, 3, 20, 21, 22, 23)
     for copy in weights:
         copy.start()
-    for out in (gg_out, gu_out, gd_out):
-        out[...] = jnp.zeros_like(out)
+    sums = (accg, accu, accd)
+    for total in sums:
+        total[...] = jnp.zeros_like(total)
     for copy in local[4:]:
         copy.wait()
 
     def stage_rows(s):
         return pl.ds(pl.multiple_of(s * ROWS, ROWS), ROWS)
 
-    def swap(s):
-        return remote(tc.at[:, 1 - core, stage_rows(s)], tx.at[:, stage_rows(s)], x_send.at[s], x_recv.at[s], partner)
+    def swap(s, t):
+        rows = stage_rows(s)
+        return remote(tc.at[t, 1 - core, rows], tx.at[t, rows], x_send.at[s, t], x_recv.at[s, t], partner)
 
     def forward_in(s):
+        swap(s, 0).wait_recv()
         slot = s % 3
         mine, other = tc[0, core, stage_rows(s), :], tx[0, stage_rows(s), :]
         for t in range(2):
@@ -130,6 +135,7 @@
             ) + jnp.dot(other, wgux[t], preferred_element_type=F32)
 
     def forward_out(s):
+        swap(s, 1).wait_recv()
         slot = s % 3
         mine, other = tc[1, core, stage_rows(s), :], tx[1, stage_rows(s), :]
         dims = (((1,), (1,)), ((), ()))
@@ -230,41 +236,49 @@
     def stage_tokens(s, t):
         return tc[t, :, stage_rows(s), :].reshape(2 * ROWS, tc.shape[-1])
 
-    def block_copy(k):
-        return remote(igb.at[:, pl.ds(BLOCK * k, BLOCK)], igr.at[k], ig_send.at[0], ig_recv.at[0], plane(*PLACES[k]))
-
-    def input_grad(s):
-        both_halves(s).wait_recv()
+    def block_copy(k, half):
+        rows = pl.ds(BLOCK * k, BLOCK)
+        late = k >= LATE
+        return remote(igb.at[half, rows], igr.at[k, half], ig_send.at[int(late)], ig_recv.at[int(late)], plane(*PLACES[k]))
+
+    def half_grad(s, half):
         dims = (((1,), (1,)), ((), ()))
-        block = lax.dot_general(stage_hidden(s, 1), wgu[0], dims, preferred_element_type=F32)
-        block = block + lax.dot_general(stage_hidden(s, 2), wgu[1], dims, preferred_element_type=F32)
-        igb[:, stage_rows(s), :] = block.astype(BF16).reshape(2, ROWS, block.shape[-1])
+        block = lax.dot_general(hid[s, half, :, ff : 2 * ff], wgu[0], dims, preferred_element_type=F32)
+        block = block + lax.dot_general(hid[s, half, :, 2 * ff :], wgu[1], dims, preferred_element_type=F32)
+        igb[half, stage_rows(s), :] = block.astype(BF16)
 
         for stage in range(STAGES):
 
             @pl.when(s == stage)
             def _():
                 for k in range(max(1, ROWS * stage // BLOCK), ROWS * (stage + 1) // BLOCK):
-                    block_copy(k).start()
+                    block_copy(k, half).start()
+
+    def input_grad(s):
+        half_grad(s, core)
+        both_halves(s).wait_recv()
+        half_grad(s, 1 - core)
 
     outer = (((0,), (0,)), ((), ()))
 
     def column_grads(s):
         left = stage_tokens(s, 0)
-        for t, out in enumerate((gg_out, gu_out)):
+        for t, out in enumerate(sums[:2]):
             out[...] += lax.dot_general(left, stage_hidden(s, t + 1), outer, preferred_element_type=F32)
 
     def down_grad(s):
-        gd_out[...] += lax.dot_general(stage_hidden(s, 0), stage_tokens(s, 1), outer, preferred_element_type=F32)
+        accd[...] += lax.dot_general(stage_hidden(s, 0), stage_tokens(s, 1), outer, preferred_element_type=F32)
 
     tokens_in(0, 1, 2, 3)
-    swap(0).start()
-    tokens_out(4, 5, 7, 8, 6, 9)
+    swap(0, 0).start()
+    tokens_out(4)
     for copy in weights[:2]:
         copy.wait_recv()
-    swap(0).wait_recv()
     forward_in(0)
     sum_send(0, 1, 0)
+    tokens_in(20, 21, 22, 23)
+    swap(0, 1).start()
+    tokens_out(5, 7, 8, 6, 9)
     weights[2].wait_recv()
     forward_out(0)
     sum_send(0, 1, 1)
@@ -282,7 +296,8 @@
             tokens_in(4, 5)
             tokens_out(12, 13, 10, 11)
             tokens_in(7, 8)
-            swap(1).start()
+            swap(1, 0).start()
+            swap(1, 1).start()
 
         @pl.when(back)
         def _():
@@ -300,9 +315,9 @@
         def _():
             sum_on(i, 1)
 
-        @pl.when(out_front)
-        def _():
-            spread_on(i - 2, 1)
+        @pl.when(grads)
+        def _():
+            down_grad(i - 4)
 
         @pl.when(i == 1)
         def _():
@@ -321,12 +336,17 @@
 
         @pl.when((i > 0) & more)
         def _():
-            swap(i + 1).start()
+            swap(i + 1, 0).start()
+            swap(i + 1, 1).start()
 
         @pl.when(back)
         def _():
             sum_on(i - 1, 3)
 
+        @pl.when(out_front)
+        def _():
+            spread_on(i - 2, 1)
+
         @pl.when(out_back)
         def _():
             spread_on(i - 3, 3)
@@ -337,7 +357,6 @@
 
         @pl.when(more)
         def _():
-            swap(i + 1).wait_recv()
             forward_in(i + 1)
             sum_send(i + 1, 1, 0)
             forward_out(i + 1)
@@ -356,27 +375,33 @@
         def _():
             spread_on(i - 3, 4)
 
-        @pl.when(grads)
-        def _():
-            down_grad(i - 4)
-
         return carry
 
     lax.fori_loop(0, STAGES + 4, step, 0)
 
-    arrived = igr.at[pl.ds(1, 15)]
-    remote(arrived, arrived, ig_send.at[0], ig_recv.at[0], partner).wait()
+    for out, total in zip((gg_out, gu_out, gd_out), sums):
+        out[...] = total[...].astype(BF16)
+
+    def arrived(first, last, late):
+        blocks = igr.at[pl.ds(first, last - first)]
+        remote(blocks, blocks, ig_send.at[late], ig_recv.at[late], partner).wait()
+
+    arrived(1, LATE, 0)
     total = igb[:, 0:BLOCK, :].astype(F32)
-    for k in range(1, 16):
+    for k in range(1, LATE):
         total = total + igr[k].astype(F32)
-    ig_out[...] = total.reshape(2 * BLOCK, total.shape[-1])
+    arrived(LATE, 16, 1)
+    for k in range(LATE, 16):
+        total = total + igr[k].astype(F32)
+    ig_out[...] = total.reshape(2 * BLOCK, total.shape[-1]).astype(BF16)
 
     for copy in a1 + weights:
         copy.wait_send()
 
     @pl.loop(0, STAGES)
     def _(s):
-        swap(s).wait_send()
+        swap(s, 0).wait_send()
+        swap(s, 1).wait_send()
 
     remote(sl, sl, ring_send.at[0], ring_send.at[0], far).wait_send()
     remote(ss, ss, ring_send.at[1], ring_send.at[1], near).wait_send()
@@ -386,11 +411,9 @@
     remote(mine, mine, pf_send.at[0], pf_send.at[0], partner).wait_send()
 
 
-def rounded(*refs):
-    wide, out, narrow, sems = refs[:4], refs[4:8], refs[8:12], refs[12]
-    copies = [pltpu.make_async_copy(b, o, sems.at[n]) for n, (b, o) in enumerate(zip(narrow, out))]
-    for a, b, copy in zip(wide, narrow, copies):
-        b[...] = a[...].astype(BF16)
+def stored(*refs):
+    copies = [pltpu.make_async_copy(refs[n], refs[4 + n], refs[8].at[n]) for n in range(4)]
+    for copy in copies:
         copy.start()
     for copy in copies:
         copy.wait()
@@ -404,10 +427,10 @@
     outs = pl.pallas_call(
         kernel,
         out_shape=(
-            pltpu.VMEM(tokens.shape, F32),
-            pltpu.VMEM((width, ff), F32),
-            pltpu.VMEM((width, ff), F32),
-            pltpu.VMEM((ff, width), F32),
+            pltpu.VMEM(tokens.shape, BF16),
+            pltpu.VMEM((width, ff), BF16),
+            pltpu.VMEM((width, ff), BF16),
+            pltpu.VMEM((ff, width), BF16),
         ),
         in_specs=[hbm] * 5,
         out_specs=(vmem,) * 4,
@@ -424,15 +447,18 @@
             pltpu.VMEM((STAGES, 3, CHUNK, 3 * ff), BF16),
             pltpu.VMEM((STAGES, 3, CHUNK, 3 * ff), BF16),
             pltpu.VMEM((STAGES, 2, ROWS, 3 * ff), BF16),
+            pltpu.VMEM((width, ff), F32),
+            pltpu.VMEM((width, ff), F32),
+            pltpu.VMEM((ff, width), F32),
             pltpu.VMEM((2, HALF, width), BF16),
             pltpu.VMEM((16, 2, BLOCK, width), BF16),
             DMA((7,)),
             DMA((3,)),
             DMA((3,)),
-            DMA((20,)),
-            DMA((20,)),
-            DMA((STAGES,)),
-            DMA((STAGES,)),
+            DMA((24,)),
+            DMA((24,)),
+            DMA((STAGES, 2)),
+            DMA((STAGES, 2)),
             DMA((4,)),
             DMA((STAGES, 4, 2)),
             DMA((STAGES, 3, 2)),
@@ -440,21 +466,21 @@
             DMA((STAGES, 3, 2)),
             DMA((1,)),
             DMA((STAGES,)),
-            DMA((1,)),
-            DMA((1,)),
+            DMA((2,)),
+            DMA((2,)),
         ],
         compiler_params=pltpu.CompilerParams(
-            collective_id=0, has_side_effects=True, vmem_limit_bytes=61300000
+            collective_id=0, has_side_effects=True, vmem_limit_bytes=64150000
         ),
     )(tokens, cotangent, gate_weight, up_weight, down_weight)
     outs = [pltpu.with_memory_space_constraint(out, pltpu.VMEM) for out in outs]
     return pl.pallas_call(
-        rounded,
+        stored,
         out_shape=tuple(jax.ShapeDtypeStruct(out.shape, BF16) for out in outs),
         in_specs=[vmem] * 4,
         out_specs=(hbm,) * 4,
-        scratch_shapes=[pltpu.VMEM(out.shape, BF16) for out in outs] + [DMA((4,))],
-        compiler_params=pltpu.CompilerParams(vmem_limit_bytes=16 * 1024 * 1024),
+        scratch_shapes=[DMA((4,))],
+        compiler_params=pltpu.CompilerParams(vmem_limit_bytes=1024 * 1024),
     )(*outs)
 
 

time: 125 us -> 124 us (level)
    pallas_call x2, Pallas kernels: 124 us -> 123 us  [the longest x1 121 us: on_device(): pl.pallas_call(kernel, out_shape=(pltpu.VMEM(tokens.shape, BF16), pltpu.V...]
where the time goes in v4:
time: 124 us
  Pallas kernels  123 us (99%)
    pallas_call x1, Pallas kernels, on_device(): pl.pallas_call(kernel, out_shape=(pltpu.VMEM(tokens.shape, BF16), pltpu.V...  121 us

profile of v4, /device:TPU:1, one launch (start us, length us, event | category | flops | bytes accessed | tf_op | source)
XLA Modules:
  0.0 123.7 jit_solution(5305369837066175997)
XLA Ops:
  0.6 121.4 %shard_map.84 = (bf16[96,512]{1,0:T(8,128)(2,1)S(1)}, bf16[512,896]{1,0:T(8,128)(2,1)S(1)}, bf16[512,896]{1,0:T(8,128)(2,1)S(1)}, bf16[896,512]{1,0:T(8,128)(2,1)S(1)}) custom-call(bf16[96,512]{1,0:T(8,128)(2,1)} %tok.1, bf16[96,512]{1,0:T(8,128)(2,1)} %cot.1, bf16[512,896]{1,0:T(8,128)(2,1)} %wg.1, bf16[512,896]{1,0:T(8,128)(2,1)} %wu.1, bf16[896,512]{1,0:T(8,128)(2,1)} %wd.1), custom_call_target="tpu_custom_call" | custom-call | tf_op jit(solution)/shard_map/pallas_call | solution.py:427
  122.1 1.6 %shard_map.85 = (bf16[96,512]{1,0:T(8,128)(2,1)}, bf16[512,896]{1,0:T(8,128)(2,1)}, bf16[512,896]{1,0:T(8,128)(2,1)}, bf16[896,512]{1,0:T(8,128)(2,1)}) custom-call(bf16[96,512]{1,0:T(8,128)(2,1)S(1)} %get-tuple-element.8.refs_0_, bf16[512,896]{1,0:T(8,128)(2,1)S(1)} %get-tuple-element.9.refs_1_, bf16[512,896]{1,0:T(8,128)(2,1)S(1)} %get-tuple-element.10.refs_2_, ...), custom_call_target="tpu_custom_call" | custom-call | tf_op jit(solution)/shard_map/pallas_call | solution.py:477

commit v5 on v4

--- a/solution.py
+++ b/solution.py
@@ -307,17 +307,13 @@
         def _():
             spread_on(i - 3, 2)
 
+        @pl.when(front)
+        def _():
+            sum_on(i, 1)
+
         @pl.when(grads)
         def _():
             input_grad(i - 4)
-
-        @pl.when(front)
-        def _():
-            sum_on(i, 1)
-
-        @pl.when(grads)
-        def _():
-            down_grad(i - 4)
 
         @pl.when(i == 1)
         def _():
@@ -342,6 +338,10 @@
         @pl.when(back)
         def _():
             sum_on(i - 1, 3)
+
+        @pl.when(grads)
+        def _():
+            down_grad(i - 4)
 
         @pl.when(out_front)
         def _():

time: 124 us -> 123 us (level)
  no operation moved by 1% of the time
where the time goes in v5:
time: 123 us
  Pallas kernels  123 us (100%)
    pallas_call x1, Pallas kernels, on_device(): pl.pallas_call(kernel, out_shape=(pltpu.VMEM(tokens.shape, BF16), pltpu.V...  121 us

profile of v5, /device:TPU:1, one launch (start us, length us, event | category | flops | bytes accessed | tf_op | source)
XLA Modules:
  0.0 123.2 jit_solution(6434296772243537162)
XLA Ops:
  0.6 120.9 %shard_map.84 = (bf16[96,512]{1,0:T(8,128)(2,1)S(1)}, bf16[512,896]{1,0:T(8,128)(2,1)S(1)}, bf16[512,896]{1,0:T(8,128)(2,1)S(1)}, bf16[896,512]{1,0:T(8,128)(2,1)S(1)}) custom-call(bf16[96,512]{1,0:T(8,128)(2,1)} %tok.1, bf16[96,512]{1,0:T(8,128)(2,1)} %cot.1, bf16[512,896]{1,0:T(8,128)(2,1)} %wg.1, bf16[512,896]{1,0:T(8,128)(2,1)} %wu.1, bf16[896,512]{1,0:T(8,128)(2,1)} %wd.1), custom_call_target="tpu_custom_call" | custom-call | tf_op jit(solution)/shard_map/pallas_call | solution.py:427
  121.6 1.6 %shard_map.85 = (bf16[96,512]{1,0:T(8,128)(2,1)}, bf16[512,896]{1,0:T(8,128)(2,1)}, bf16[512,896]{1,0:T(8,128)(2,1)}, bf16[896,512]{1,0:T(8,128)(2,1)}) custom-call(bf16[96,512]{1,0:T(8,128)(2,1)S(1)} %get-tuple-element.8.refs_0_, bf16[512,896]{1,0:T(8,128)(2,1)S(1)} %get-tuple-element.9.refs_1_, bf16[512,896]{1,0:T(8,128)(2,1)S(1)} %get-tuple-element.10.refs_2_, ...), custom_call_target="tpu_custom_call" | custom-call | tf_op jit(solution)/shard_map/pallas_call | solution.py:477
